TPU v7x, 256 devices: a whole 4x4x8 slice. The times are simulated.
256 devices in a mesh: term: 4 (over x), sector: 64 (over y, z, core).
Axes of the slice: x: 4, y: 4, z: 8, core: 2. Of those that a mesh axis runs over, the one named last changes fastest.
Arguments:
- psi_blocks: bfloat16 [4096, 128, 128], P('sector'), may hold values from -6 to 6
- right_ops: bfloat16 [8, 4096, 128, 128], P('term', 'sector'), may hold values from -0.5 to 0.5
- left_ops: bfloat16 [8, 4096, 128, 128], P('term', 'sector'), may hold values from -0.1875 to 0.1875
- owner_map: int32 [4096, 1], P('sector'), may hold values from 0 to 63; in each aligned block of 64 rows (0 to 63, 64 to 127, ...) at most 2 rows name the same one
- left_local: int32 [4096, 1], P('sector'), may hold values from 0 to 63
Outputs:
- sigma: bfloat16 [4096, 128, 128], P('sector', 'term')
Inputs may be any that keep to these rules, and one draw needn't show every extreme that they name: `owner_map`: among the 64 sectors held by one device along `sector` (aligned blocks), at most 2 name the same owner; some block reaches it.
All inputs are finite; a program needn't handle non-finite values.
Results may differ from a plain program's by a relative error of at most 0.0049.
Values may be sent and summed in bfloat16 or wider, within the bound.
A program may use at most 128 MiB of HBM per device.

v0:
```python
import jax
import jax.numpy as jnp
from jax import lax
from jax.sharding import PartitionSpec as P


def ranks_of(owners):
    count = owners.shape[-1]
    same = owners[..., :, None] == owners[..., None, :]
    earlier = lax.broadcasted_iota(jnp.int32, (count, count), 0) < lax.broadcasted_iota(
        jnp.int32, (count, count), 1
    )
    return jnp.sum((same & earlier).astype(jnp.int32), axis=-2)


def local(psi_blocks, right_ops, left_ops, owner_map, left_local):
    sec_dev = psi_blocks.shape[0]
    width = psi_blocks.shape[1]
    terms_dev = right_ops.shape[0]
    n_sector = lax.axis_size("sector")
    capacity = max(2, 2 * sec_dev // n_sector)
    slots = n_sector * capacity
    owners = owner_map[:, 0]
    slot_id = owners * capacity + ranks_of(owners)
    packer = (lax.broadcasted_iota(jnp.int32, (slots, sec_dev), 0) == slot_id[None, :]).astype(
        jnp.bfloat16
    )
    routes_all = lax.all_gather(
        jnp.concatenate([owner_map, left_local], axis=1), "sector", axis=0, tiled=True
    )
    all_owners = routes_all[:, 0].reshape(n_sector, sec_dev)
    all_local = routes_all[:, 1].reshape(n_sector, sec_dev)
    all_ranks = ranks_of(all_owners)
    mine = lax.axis_index("sector")
    slot_iota = lax.broadcasted_iota(jnp.int32, (1, 1, capacity), 2)
    hits = (all_owners == mine)[:, :, None] & (all_ranks[:, :, None] == slot_iota)
    tags = (jnp.sum(jnp.where(hits, all_local[:, :, None] + 1, 0), axis=1) - 1).reshape(slots)
    inter = jnp.einsum(
        "sij,tsjk->stik", psi_blocks, right_ops, preferred_element_type=jnp.float32
    ).astype(jnp.bfloat16)
    packed = jnp.dot(packer, inter.reshape(sec_dev, -1), preferred_element_type=jnp.float32).astype(
        jnp.bfloat16
    )
    arrived = lax.all_to_all(
        packed.reshape(n_sector, capacity, -1), "sector", split_axis=0, concat_axis=0, tiled=True
    )
    arrived = arrived.reshape(slots, terms_dev, width, width)
    picked = jnp.take(left_ops, jnp.clip(tags, 0, sec_dev - 1), axis=1)
    images = jnp.einsum("tnij,ntjk->nik", picked, arrived, preferred_element_type=jnp.float32)
    collect = (lax.broadcasted_iota(jnp.int32, (sec_dev, slots), 0) == tags[None, :]).astype(
        jnp.float32
    )
    partial_sum = jnp.dot(
        collect,
        images.reshape(slots, -1),
        precision=lax.Precision.HIGHEST,
        preferred_element_type=jnp.float32,
    ).reshape(sec_dev, width, width)
    total = lax.psum(partial_sum, "term")
    row_count = width // lax.axis_size("term")
    mine_rows = lax.dynamic_slice_in_dim(total, lax.axis_index("term") * row_count, row_count, 1)
    return mine_rows.astype(jnp.bfloat16)


def solution(mesh):
    placed = (
        P("sector", None, None),
        P("term", "sector", None, None),
        P("term", "sector", None, None),
        P("sector", None),
        P("sector", None),
    )
    return jax.shard_map(
        local, mesh=mesh, in_specs=placed, out_specs=P("sector", "term", None), check_vma=False
    )
```

profile of v0, /device:TPU:1, one launch (start us, length us, event | category | flops | bytes accessed | tf_op | source)
XLA Modules:
  0.0 411.3 jit_solution(9655905848802338681)
XLA Ops:
  0.0 0.0 copy-start
  0.0 0.9 convert_reduce_fusion.1
  0.9 0.7 multiply_add_fusion
  1.6 0.0 copy-done
  1.6 5.4 %convert_bitcast_fusion = bf16[64,2,128,128]{2,3,1,0:T(8,128)(2,1)} fusion(bf16[2,64,128,128]{3,2,1,0:T(8,128)(2,1)} %param.6, bf16[64,128,128]{2,1,0:T(8,128)(2,1)S(1)} %copy-done), kind=kOutput, calls=%fused_computation.12 | convolution fusion | flops 538968064 | bytes 10485760 | tf_op jit(solution)/shard_map/sij,tsjk->stik/dot_general | solution.py:38
  7.0 6.3 %copy.23 = bf16[64,2,128,128]{3,2,1,0:T(8,128)(2,1)} copy(bf16[64,2,128,128]{2,3,1,0:T(8,128)(2,1)} %convert_bitcast_fusion) | data formatting | bytes 8388608 | tf_op jit(solution)/shard_map/convert_element_type | solution.py:40
  13.4 8.8 %convolution_convert_fusion = bf16[128,32768]{1,0:T(8,128)(2,1)} fusion(bf16[8,8,256,128]{3,2,1,0:T(8,128)(2,1)} %bitcast.41, s32[64]{0:T(128)S(1)} %multiply_add_fusion), kind=kOutput, calls=%fused_computation.1 | convolution fusion | flops 541073408 | bytes 12583168 | tf_op jit(solution)/shard_map/dot_general | solution.py:41
  22.1 14.1 %reshape.90 = bf16[64,2,32768]{2,1,0:T(2,128)(2,1)} reshape(bf16[128,32768]{1,0:T(8,128)(2,1)} %convolution_convert_fusion) | data formatting | bytes 16777216 | tf_op jit(solution)/shard_map/reshape | solution.py:45
  36.3 13.5 %all-to-all-start = ((bf16[64,2,32768]{2,1,0:T(2,128)(2,1)}), bf16[64,2,32768]{2,1,0:T(2,128)(2,1)}, u32[]{:S(2)}, u32[]{:S(2)}) async-start(bf16[64,2,32768]{2,1,0:T(2,128)(2,1)} %reshape.90), calls=%async_computation | async-start | bytes 16777216 | tf_op jit(solution)/shard_map/all_to_all | solution.py:44
  49.8 0.0 copy-done.2
  49.8 0.0 copy-done.3
  49.8 218.2 %all-gather = s32[64,64,2]{1,2,0:T(2,128)S(1)} all-gather(s32[1,64,2]{1,2,0:T(2,128)S(1)} %add_bitcast_fusion), channel_id=1, replica_groups=mesh['term'=4,'sector'=64] {'sector'}, dimensions={0}, use_global_device_ids=true | all-gather | bytes 33280 | tf_op jit(solution)/shard_map/all_gather | solution.py:28
  268.0 0.1 reshape.102
  268.1 0.1 slice_reduce_fusion
  268.2 0.1 reshape_squeeze.3
  268.3 0.1 add.66
  268.4 0.9 convert_reduce_fusion
  269.3 0.1 select_reduce_fusion
  269.4 0.1 copy.20
  269.5 0.1 sub.7
  269.7 0.1 copy.21
  269.8 0.1 min.18
  269.9 8.6 %gather_fusion = bf16[128,2,128,128]{3,2,1,0:T(8,128)(2,1)} fusion(bf16[2,64,128,128]{3,2,1,0:T(8,128)(2,1)} %param.7, s32[1024]{0:T(1024)S(1)} %pad_clamp_fusion), kind=kCustom, calls=%fused_computation | custom fusion | bytes 16777728 | tf_op jit(solution)/shard_map/jit(_take)/gather | solution.py:48
  278.5 0.0 all-to-all-done
  278.5 14.6 %reshape.91 = bf16[128,2,128,128]{3,2,1,0:T(8,128)(2,1)} reshape(bf16[64,2,32768]{2,1,0:T(2,128)(2,1)} %all-to-all-done) | data formatting | bytes 16777216 | tf_op jit(solution)/shard_map/reshape | solution.py:47
  293.1 8.2 %fusion = f32[128,128,128,1]{2,1,3,0:T(8,128)S(1)} fusion(bf16[128,2,128,128]{3,2,1,0:T(8,128)(2,1)} %reshape.91, bf16[128,2,128,128]{3,2,1,0:T(8,128)(2,1)} %gather_fusion, pred[128]{0:T(512)(128)(4,1)S(1)} %compare_and_fusion), kind=kOutput, calls=%fused_computation.3 | convolution fusion | flops 1077936128 | bytes 25165952 | tf_op jit(solution)/shard_map/tnij,ntjk->nik/dot_general | solution.py:49
  301.3 9.7 %copy.41 = f32[16,8,128,128]{3,1,2,0:T(8,128)} copy(f32[16,8,128,128]{3,2,1,0:T(8,128)S(1)} %bitcast.38) | data formatting | bytes 16777216
  311.1 9.0 %copy.24 = f32[16384,128]{1,0:T(8,128)} copy(f32[16384,128]{0,1:T(8,128)} %bitcast.40) | data formatting | bytes 16777216 | tf_op jit(solution)/shard_map/dot_general | solution.py:53
  320.1 10.5 %fusion.15 = f32[64,128,128]{2,0,1:T(8,128)} fusion(f32[128,128,128]{2,1,0:T(8,128)} %bitcast.39, s32[128]{0:T(128)S(1)} %sub.7), kind=kOutput, calls=%fused_computation.25 | convolution fusion | flops 1610620928 | bytes 12583424 | tf_op jit(solution)/shard_map/dot_general | solution.py:53
  330.6 78.5 %all-reduce.1 = bf16[64,128,128]{2,0,1:T(8,128)(2,1)} all-reduce(f32[64,128,128]{2,0,1:T(8,128)} %fusion.15), channel_id=1, replica_groups=mesh['term'=4,'sector'=64] {'term'}, use_global_device_ids=true, to_apply=%region_3.4 | all-reduce | flops 1048576 | bytes 6291456 | tf_op jit(solution)/shard_map/psum | solution.py:59
  409.1 1.1 dynamic-slice_convert_fusion
  410.2 1.1 copy.25
  (12 shorter events, 0.1 us)
Async XLA Ops:
  0.0 1.6 copy-start
  36.3 13.5 %copy-start.2 = (s32[64,1]{0,1:T(1,128)S(1)}, s32[64,1]{0,1:T(1,128)}, u32[]{:S(2)}) copy-start(s32[64,1]{0,1:T(1,128)} %param.8) | copy-start | bytes 772
  36.3 13.5 %copy-start.3 = (s32[64,1]{0,1:T(1,128)S(1)}, s32[64,1]{0,1:T(1,128)}, u32[]{:S(2)}) copy-start(s32[64,1]{0,1:T(1,128)} %param.9) | copy-start | bytes 772
  36.3 242.2 %all-to-all-start = ((bf16[64,2,32768]{2,1,0:T(2,128)(2,1)}), bf16[64,2,32768]{2,1,0:T(2,128)(2,1)}, u32[]{:S(2)}, u32[]{:S(2)}) async-start(bf16[64,2,32768]{2,1,0:T(2,128)(2,1)} %reshape.90), calls=%async_computation | async-start | bytes 16777216 | tf_op jit(solution)/shard_map/all_to_all | solution.py:44
  320.1 91.2 %copy-start.1 = (bf16[64,128,128]{2,1,0:T(8,128)(2,1)S(1)}, bf16[64,128,128]{2,1,0:T(8,128)(2,1)}, u32[]{:S(2)}) copy-start(bf16[64,128,128]{2,1,0:T(8,128)(2,1)} %param.5) | copy-start | bytes 6291460
where the time goes:
time: 413 us; the launch traced here: 411 us
  blocking collectives  297 us (72%)
  local copies, waits for them, and re-layouts  65.4 us (16%)
  matrix products  32.9 us (8%)
  starting transfers between devices  13.5 us (3%)
    all_gather x1, blocking collectives, local(): lax.all_gather(jnp.concatenate([owner_map, left_local], axis=1), 'sector'...  218 us
    psum x1, blocking collectives, local(): total = lax.psum(partial_sum, 'term')  78.5 us
    reshape x1, local copies, waits for them, and re-layouts, local(): arrived = arrived.reshape(slots, terms_dev, width, width)  14.6 us
    reshape x1, local copies, waits for them, and re-layouts, local(): packed.reshape(n_sector, capacity, -1)  14.1 us
    all_to_all x1, starting transfers between devices, local(): lax.all_to_all(packed.reshape(n_sector, capacity, -1), 'sector', split_ax...  13.5 us
    dot_general x1, matrix products, local(): jnp.dot(collect, images.reshape(slots, -1), precision=lax.Precision.HIGHE...  10.5 us
    unnamed x10, local copies, waits for them, and re-layouts  9.9 us
    dot_general x1, local copies, waits for them, and re-layouts, local(): jnp.dot(collect, images.reshape(slots, -1), precision=lax.Precision.HIGHE...  8.99 us
  transfers between devices with their start and end apart: 1, of which 0 were waited for; matrix products, arithmetic and copies ran while one was open for 3% of the time, Pallas kernels for 0%

commit v1 on v0

--- a/solution.py
+++ b/solution.py
@@ -14,6 +14,18 @@
 
 
 def local(psi_blocks, right_ops, left_ops, owner_map, left_local):
+
+    def _put_trees(vec):
+        device_axis = "term"
+        chips = lax.psum(1, device_axis)
+        state_now = vec
+        response = lambda y_new: [(dev, dev ^ y_new) for dev in range(chips)]
+        for num in range(chips.bit_length() - 1):
+            built = response(1 << num)
+            out_arr = lax.ppermute(state_now, device_axis, built)
+            state_now = state_now + out_arr
+        return state_now
+
     sec_dev = psi_blocks.shape[0]
     width = psi_blocks.shape[1]
     terms_dev = right_ops.shape[0]
@@ -56,7 +68,7 @@
         precision=lax.Precision.HIGHEST,
         preferred_element_type=jnp.float32,
     ).reshape(sec_dev, width, width)
-    total = lax.psum(partial_sum, "term")
+    total = _put_trees(partial_sum)
     row_count = width // lax.axis_size("term")
     mine_rows = lax.dynamic_slice_in_dim(total, lax.axis_index("term") * row_count, row_count, 1)
     return mine_rows.astype(jnp.bfloat16)

time: 413 us -> 520 us (1.26)
  waiting for transfers between devices: 0.01 us -> 181 us
  blocking collectives: 297 us -> 218 us
    ppermute x0 -> x2, waiting for transfers between devices: none -> 181 us  [_put_trees(): out_arr = lax.ppermute(state_now, device_axis, built)]
    psum x1 -> x0, blocking collectives: 78.5 us -> none  [local(): total = lax.psum(partial_sum, 'term')]
  transfers between devices with their start and end apart: 1 -> 3, of which waited for: 0 -> 2; matrix products, arithmetic and copies ran while one was open for 3% -> 2% of each run, Pallas kernels for 0% -> 0%
where the time goes in v1:
time: 520 us; the launch traced here: 518 us
  blocking collectives  218 us (42%)
  waiting for transfers between devices  181 us (35%)
  local copies, waits for them, and re-layouts  64.3 us (12%)
  matrix products  29.7 us (6%)
  starting transfers between devices  17.5 us (3%)
  other arithmetic  7.32 us (1%)
    all_gather x1, blocking collectives, local(): lax.all_gather(jnp.concatenate([owner_map, left_local], axis=1), 'sector'...  218 us
    ppermute x2, waiting for transfers between devices, _put_trees(): out_arr = lax.ppermute(state_now, device_axis, built)  181 us
    reshape x1, local copies, waits for them, and re-layouts, local(): arrived = arrived.reshape(slots, terms_dev, width, width)  14.6 us
    reshape x1, local copies, waits for them, and re-layouts, local(): packed.reshape(n_sector, capacity, -1)  14.1 us
    all_to_all x1, starting transfers between devices, local(): lax.all_to_all(packed.reshape(n_sector, capacity, -1), 'sector', split_ax...  13.5 us
  transfers between devices with their start and end apart: 3, of which 2 were waited for; matrix products, arithmetic and copies ran while one was open for 2% of the time, Pallas kernels for 0%

profile of v1, /device:TPU:1, one launch (start us, length us, event | category | flops | bytes accessed | tf_op | source)
XLA Modules:
  0.0 518.1 jit_solution(12275244872856782721)
XLA Ops:
  0.0 0.9 convert_reduce_fusion.1
  0.9 0.7 multiply_add_fusion
  1.6 0.0 copy-done
  1.6 5.4 %convert_bitcast_fusion = bf16[64,2,128,128]{2,3,1,0:T(8,128)(2,1)} fusion(bf16[2,64,128,128]{3,2,1,0:T(8,128)(2,1)} %param.6, bf16[64,128,128]{2,1,0:T(8,128)(2,1)S(1)} %copy-done), kind=kOutput, calls=%fused_computation.12 | convolution fusion | flops 538968064 | bytes 10485760 | tf_op jit(solution)/shard_map/sij,tsjk->stik/dot_general | solution.py:50
  7.0 6.3 %copy.23 = bf16[64,2,128,128]{3,2,1,0:T(8,128)(2,1)} copy(bf16[64,2,128,128]{2,3,1,0:T(8,128)(2,1)} %convert_bitcast_fusion) | data formatting | bytes 8388608 | tf_op jit(solution)/shard_map/convert_element_type | solution.py:52
  13.4 8.8 %convolution_convert_fusion = bf16[128,32768]{1,0:T(8,128)(2,1)} fusion(bf16[8,8,256,128]{3,2,1,0:T(8,128)(2,1)} %bitcast.41, s32[64]{0:T(128)S(1)} %multiply_add_fusion), kind=kOutput, calls=%fused_computation.1 | convolution fusion | flops 541073408 | bytes 12583168 | tf_op jit(solution)/shard_map/dot_general | solution.py:53
  22.1 14.1 %reshape.90 = bf16[64,2,32768]{2,1,0:T(2,128)(2,1)} reshape(bf16[128,32768]{1,0:T(8,128)(2,1)} %convolution_convert_fusion) | data formatting | bytes 16777216 | tf_op jit(solution)/shard_map/reshape | solution.py:57
  36.3 13.5 %all-to-all-start = ((bf16[64,2,32768]{2,1,0:T(2,128)(2,1)}), bf16[64,2,32768]{2,1,0:T(2,128)(2,1)}, u32[]{:S(2)}, u32[]{:S(2)}) async-start(bf16[64,2,32768]{2,1,0:T(2,128)(2,1)} %reshape.90), calls=%async_computation | async-start | bytes 16777216 | tf_op jit(solution)/shard_map/all_to_all | solution.py:56
  49.8 218.2 %all-gather = s32[64,64,2]{1,2,0:T(2,128)S(1)} all-gather(s32[1,64,2]{1,2,0:T(2,128)S(1)} %add_bitcast_fusion), channel_id=1, replica_groups=mesh['term'=4,'sector'=64] {'sector'}, dimensions={0}, use_global_device_ids=true | all-gather | bytes 33280 | tf_op jit(solution)/shard_map/all_gather | solution.py:40
  268.0 0.1 reshape.102
  268.1 0.1 slice_reduce_fusion
  268.2 0.1 reshape_squeeze.3
  268.3 0.1 add.70
  268.4 0.9 convert_reduce_fusion
  269.3 0.1 select_reduce_fusion
  269.4 0.1 copy.20
  269.5 0.1 sub.7
  269.7 0.1 copy.21
  269.8 0.1 min.18
  269.9 8.6 %gather_fusion = bf16[128,2,128,128]{3,2,1,0:T(8,128)(2,1)} fusion(bf16[2,64,128,128]{3,2,1,0:T(8,128)(2,1)} %param.7, s32[1024]{0:T(1024)S(1)} %pad_clamp_fusion), kind=kCustom, calls=%fused_computation | custom fusion | bytes 16777728 | tf_op jit(solution)/shard_map/jit(_take)/gather | solution.py:60
  278.5 14.6 %reshape.91 = bf16[128,2,128,128]{3,2,1,0:T(8,128)(2,1)} reshape(bf16[64,2,32768]{2,1,0:T(2,128)(2,1)} %all-to-all-done) | data formatting | bytes 16777216 | tf_op jit(solution)/shard_map/reshape | solution.py:59
  293.1 8.2 %fusion = f32[128,128,128,1]{2,1,3,0:T(8,128)S(1)} fusion(bf16[128,2,128,128]{3,2,1,0:T(8,128)(2,1)} %reshape.91, bf16[128,2,128,128]{3,2,1,0:T(8,128)(2,1)} %gather_fusion, pred[128]{0:T(512)(128)(4,1)S(1)} %compare_and_fusion), kind=kOutput, calls=%fused_computation.3 | convolution fusion | flops 1077936128 | bytes 25165952 | tf_op jit(solution)/shard_map/tnij,ntjk->nik/dot_general | solution.py:61
  301.3 9.8 %copy.41 = f32[16,8,128,128]{3,1,2,0:T(8,128)} copy(f32[16,8,128,128]{3,2,1,0:T(8,128)S(1)} %bitcast.38) | data formatting | bytes 16777216
  311.1 9.0 %copy.24 = f32[16384,128]{1,0:T(8,128)} copy(f32[16384,128]{0,1:T(8,128)} %bitcast.40) | data formatting | bytes 16777216 | tf_op jit(solution)/shard_map/dot_general | solution.py:65
  320.1 7.4 %fusion.16 = f32[64,128,128]{2,0,1:T(8,128)S(1)} fusion(f32[128,128,128]{2,1,0:T(8,128)} %bitcast.39, s32[128]{0:T(128)S(1)} %sub.7), kind=kOutput, calls=%fused_computation.26 | convolution fusion | flops 1610620928 | bytes 12583424 | tf_op jit(solution)/shard_map/dot_general | solution.py:65
  327.4 1.3 collective-permute-start
  328.7 90.7 %collective-permute-done = f32[64,128,128]{2,0,1:T(8,128)S(1)} collective-permute-done((f32[64,128,128]{2,0,1:T(8,128)S(1)}, f32[64,128,128]{2,0,1:T(8,128)S(1)}, u32[]{:S(2)}, u32[]{:S(2)}) %collective-permute-start) | collective-permute-done | bytes 4194336 | tf_op jit(solution)/shard_map/ppermute | solution.py:25
  419.5 2.9 add.76
  422.4 2.7 collective-permute-start.1
  425.1 90.2 %collective-permute-done.1 = f32[64,128,128]{2,0,1:T(8,128)} collective-permute-done((f32[64,128,128]{2,0,1:T(8,128)}, f32[64,128,128]{2,0,1:T(8,128)}, u32[]{:S(2)}, u32[]{:S(2)}) %collective-permute-start.1) | collective-permute-done | bytes 4194336 | tf_op jit(solution)/shard_map/ppermute | solution.py:25
  515.3 1.7 fusion.12
  517.0 1.1 copy.25
  (16 shorter events, 0.1 us)
Async XLA Ops:
  0.0 1.6 copy-start
  36.3 13.5 %copy-start.2 = (s32[64,1]{0,1:T(1,128)S(1)}, s32[64,1]{0,1:T(1,128)}, u32[]{:S(2)}) copy-start(s32[64,1]{0,1:T(1,128)} %param.8) | copy-start | bytes 772
  36.3 13.5 %copy-start.3 = (s32[64,1]{0,1:T(1,128)S(1)}, s32[64,1]{0,1:T(1,128)}, u32[]{:S(2)}) copy-start(s32[64,1]{0,1:T(1,128)} %param.9) | copy-start | bytes 772
  36.3 242.2 %all-to-all-start = ((bf16[64,2,32768]{2,1,0:T(2,128)(2,1)}), bf16[64,2,32768]{2,1,0:T(2,128)(2,1)}, u32[]{:S(2)}, u32[]{:S(2)}) async-start(bf16[64,2,32768]{2,1,0:T(2,128)(2,1)} %reshape.90), calls=%async_computation | async-start | bytes 16777216 | tf_op jit(solution)/shard_map/all_to_all | solution.py:56
  327.4 92.0 %collective-permute-start = (f32[64,128,128]{2,0,1:T(8,128)S(1)}, f32[64,128,128]{2,0,1:T(8,128)S(1)}, u32[]{:S(2)}, u32[]{:S(2)}) collective-permute-start(f32[64,128,128]{2,0,1:T(8,128)S(1)} %fusion.16), channel_id=1, source_target_pairs={{0,64},{64,0},{128,192},{192,128},{1,65},{65,1},{129,193},{193,129... | collective-permute-start | bytes 12582920 | tf_op jit(solution)/shard_map/ppermute | solution.py:25
  419.5 98.7 %copy-start.1 = (bf16[64,128,128]{2,1,0:T(8,128)(2,1)S(1)}, bf16[64,128,128]{2,1,0:T(8,128)(2,1)}, u32[]{:S(2)}) copy-start(bf16[64,128,128]{2,1,0:T(8,128)(2,1)} %param.5) | copy-start | bytes 6291460
  422.4 92.9 %collective-permute-start.1 = (f32[64,128,128]{2,0,1:T(8,128)}, f32[64,128,128]{2,0,1:T(8,128)}, u32[]{:S(2)}, u32[]{:S(2)}) collective-permute-start(f32[64,128,128]{2,0,1:T(8,128)} %add.76), channel_id=1, source_target_pairs={{0,128},{64,192},{128,0},{192,64},{1,129},{65,193},{129,1},{193,65... | collective-permute-start | bytes 12582920 | tf_op jit(solution)/shard_map/ppermute | solution.py:25
